TPU v7x, 32 devices: a whole 2x2x4 slice. The times are simulated.
32 devices in a mesh: dp: 2 (over x), ctx: 16 (over z, y, core).
Axes of the slice: x: 2, y: 2, z: 4, core: 2. Of those that a mesh axis runs over, the one named last changes fastest.
Arguments:
- queries: bfloat16 [2, 6144, 4096], P('dp', 'ctx'), may hold values from -6 to 6
- keys: bfloat16 [2, 6144, 4096], P('dp', 'ctx'), may hold values from -6 to 6
- values: bfloat16 [2, 6144, 4096], P('dp', 'ctx'), may hold values from -6 to 6
- out_grad: bfloat16 [2, 6144, 4096], P('dp', 'ctx'), may hold values from -15 to 15
- gain: float32 [4096], replicated, may hold values from 0.1 to 1.9
Outputs:
- output: bfloat16 [2, 6144, 4096], P('dp', 'ctx')
- grad_queries: bfloat16 [2, 6144, 4096], P('dp', 'ctx')
- grad_keys: bfloat16 [2, 6144, 4096], P('dp', 'ctx')
- grad_values: bfloat16 [2, 6144, 4096], P('dp', 'ctx')
- grad_gain: float32 [4096], replicated
All inputs are finite; a program needn't handle non-finite values.
Results may differ from a plain program's by a relative error of at most 0.007.
Values sent between devices are 32-bit elements; how exact they have to be, the bound alone decides.
A program may use at most 256 MiB of HBM per device.

v0:
```python
import jax
import jax.numpy as jnp
from jax import lax
from jax.sharding import PartitionSpec as P

HD = 128


EPS = 1e-06


def entering(x, axis, combine, identity, reverse):
    size, position = (lax.axis_size(axis), lax.axis_index(axis))
    everything = lax.all_gather(x, axis)
    start = jnp.broadcast_to(jnp.asarray(identity, x.dtype), x.shape)

    def lap(k, before):
        at = size - 1 - k if reverse else k
        reached = at > position if reverse else at < position
        new = combine(before, everything[at])
        return jnp.where(reached, new, before)

    return lax.fori_loop(0, size, lap, start)


def add_states(earlier, later):
    return earlier + later


def body(queries, keys, values, out_grad, gain):
    length = queries.shape[1]
    heads = gain.shape[0] // HD
    query = queries[0].reshape(length, heads, HD)
    key_rows = keys[0].reshape(length, heads, HD)
    value = values[0].reshape(length, heads, HD)
    gain_rows = gain.reshape(heads, HD)
    row_index = lax.broadcasted_iota(jnp.int32, (length, length), 0)
    col_index = lax.broadcasted_iota(jnp.int32, (length, length), 1)
    causal = (row_index >= col_index)[None]
    local_state = jnp.einsum("jhd,jhe->hde", key_rows, value, preferred_element_type=jnp.float32)
    empty = jnp.zeros_like(local_state)
    prefix = entering(local_state, "ctx", add_states, empty, False)
    prefix_bf = prefix.astype(jnp.bfloat16)
    scores = jnp.einsum("ihd,jhd->hij", query, key_rows, preferred_element_type=jnp.float32)
    scores = jnp.where(causal, scores, 0.0).astype(jnp.bfloat16)
    attended = jnp.einsum("hij,jhe->ihe", scores, value, preferred_element_type=jnp.float32)
    attended = attended + jnp.einsum(
        "ihd,hde->ihe", query, prefix_bf, preferred_element_type=jnp.float32
    )
    inverse = lax.rsqrt(jnp.mean(attended * attended, axis=-1, keepdims=True) + EPS)
    normed = attended * inverse
    output = (normed * gain_rows).astype(jnp.bfloat16)
    grad_float = out_grad[0].reshape(length, heads, HD).astype(jnp.float32)
    gain_term = jnp.sum(grad_float * normed, axis=0)
    scaled = grad_float * gain_rows
    dattn = (
        inverse * (scaled - normed * jnp.mean(scaled * normed, axis=-1, keepdims=True))
    ).astype(jnp.bfloat16)
    gstate = jnp.einsum("ihd,ihe->hde", query, dattn, preferred_element_type=jnp.float32)
    suffix = entering(gstate, "ctx", add_states, empty, True)
    suffix_bf = suffix.astype(jnp.bfloat16)
    dscore = jnp.einsum("ihe,jhe->hij", dattn, value, preferred_element_type=jnp.float32)
    dscore = jnp.where(causal, dscore, 0.0).astype(jnp.bfloat16)
    grad_q = jnp.einsum("hij,jhd->ihd", dscore, key_rows, preferred_element_type=jnp.float32)
    grad_q = grad_q + jnp.einsum(
        "ihe,hde->ihd", dattn, prefix_bf, preferred_element_type=jnp.float32
    )
    grad_k = jnp.einsum("hij,ihd->jhd", dscore, query, preferred_element_type=jnp.float32)
    grad_k = grad_k + jnp.einsum(
        "jhe,hde->jhd", value, suffix_bf, preferred_element_type=jnp.float32
    )
    grad_v = jnp.einsum("hij,ihe->jhe", scores, dattn, preferred_element_type=jnp.float32)
    grad_v = grad_v + jnp.einsum(
        "jhd,hde->jhe", key_rows, suffix_bf, preferred_element_type=jnp.float32
    )
    grad_gain = lax.psum(gain_term.reshape(heads * HD), ("dp", "ctx"))
    flat_shape = (1, length, heads * HD)
    return (
        output.reshape(flat_shape),
        grad_q.astype(jnp.bfloat16).reshape(flat_shape),
        grad_k.astype(jnp.bfloat16).reshape(flat_shape),
        grad_v.astype(jnp.bfloat16).reshape(flat_shape),
        grad_gain,
    )


def solution(mesh):
    placed = (
        P("dp", "ctx", None),
        P("dp", "ctx", None),
        P("dp", "ctx", None),
        P("dp", "ctx", None),
        P(),
    )
    return jax.shard_map(
        body,
        mesh=mesh,
        in_specs=placed,
        out_specs=(
            P("dp", "ctx", None),
            P("dp", "ctx", None),
            P("dp", "ctx", None),
            P("dp", "ctx", None),
            P(),
        ),
        check_vma=False,
    )
```

profile of v0, /device:TPU:0, one launch (start us, length us, event | category | flops | bytes accessed | tf_op | source)
XLA Modules:
  0.0 508.8 jit_solution(7686650805659091087)
XLA Ops:
  7.2 4.4 copy.59
  11.6 3.8 copy.35
  15.4 3.9 copy.60
  19.3 1.6 copy-done.1
  20.9 3.8 fusion.10
  24.7 0.3 all-gather.7.cloned.1.call-start
  25.0 4.4 copy.58
  29.4 5.4 %copy.39 = f32[1,384,4096]{1,2,0:T(8,128)} copy(bf16[1,384,4096]{2,1,0:T(8,128)(2,1)} %param.12) | data formatting | bytes 9437184 | tf_op jit(solution)/shard_map/convert_element_type | solution.py:53
  34.8 13.7 %select_convert_fusion.1 = bf16[32,384,384]{2,1,0:T(8,128)(2,1)} fusion(pred[384,384]{1,0:T(8,128)(4,1)S(1)} %iota_compare_fusion, bf16[384,32,128]{2,1,0:T(8,128)(2,1)} %bitcast.69, bf16[384,32,128]{2,1,0:T(8,128)(2,1)} %bitcast.64), kind=kOutput, calls=%fused_computation.3 | convolution fusion | flops 1217396736 | bytes 15876096 | tf_op jit(solution)/shard_map/ihd,jhd->hij/dot_general | solution.py:44
  48.5 11.6 %fusion.5 = f32[32,384,128]{1,2,0:T(8,128)} fusion(bf16[32,384,384]{2,1,0:T(8,128)(2,1)} %select_convert_fusion.1, bf16[384,32,128]{2,1,0:T(8,128)(2,1)} %bitcast.61), kind=kOutput, calls=%fused_computation.18 | convolution fusion | flops 1207959552 | bytes 18874368 | tf_op jit(solution)/shard_map/hij,jhe->ihe/dot_general | solution.py:46
  60.0 135.6 %all-gather.5.cloned.1.call-done = f32[512,128,128]{2,1,0:T(8,128)} async-done(((f32[32,128,128]{2,1,0:T(8,128)}), f32[512,128,128]{2,1,0:T(8,128)}) %all-gather.5.cloned.1.call-update) | async-done | bytes 33554448 | tf_op jit(solution)/shard_map/all_gather | solution.py:14
  195.6 37.6 %while.30 = (s32[]{:T(128)}, f32[32,128,128]{2,1,0:T(8,128)S(1)}, s32[]{:T(128)}, f32[16,32,128,128]{3,2,1,0:T(8,128)}, s32[]{:T(128)}, /*index=5*/s32[]{:T(128)}) while((s32[]{:T(128)}, f32[32,128,128]{2,1,0:T(8,128)S(1)}, s32[]{:T(128)}, f32[16,32,128,128]{3,2,1,0:T(8,128)}, s32[]{:T(128)}, /*index=5*/s32[]{:T(128)}) %tuple.89), condition=%wide.region_1.2_spmd.clone, body=%wide.region_0.1_spmd.clone.sunk | while | flops 1572868 | bytes 6291557 | solution.py:23
  195.9 2.3 add_select_fusion.4
  198.2 2.3 add_select_fusion.4
  200.6 2.3 add_select_fusion.4
  202.9 2.3 add_select_fusion.4
  205.2 2.3 add_select_fusion.4
  207.6 2.3 add_select_fusion.4
  209.9 2.3 add_select_fusion.4
  212.2 2.3 add_select_fusion.4
  214.6 2.3 add_select_fusion.4
  216.9 2.3 add_select_fusion.4
  219.3 2.3 add_select_fusion.4
  221.6 2.3 add_select_fusion.4
  223.9 2.3 add_select_fusion.4
  226.3 2.3 add_select_fusion.4
  228.6 2.3 add_select_fusion.4
  230.9 2.3 add_select_fusion.4
  233.3 7.7 %multiply_reduce_fusion.2 = (f32[384,32]{0,1:T(8,128)S(1)}, f32[384,32,128]{0,2,1:T(8,128)S(1)}) fusion(bf16[384,32,128]{2,1,0:T(8,128)(2,1)} %bitcast.65, f32[32,128,128]{2,1,0:T(8,128)S(1)} %get-tuple-element.194, f32[32,384,128]{1,2,0:T(8,128)} %fusion.5), kind=kOutput, calls=%fused_computation.14 | convolution fusion | flops 407883776 | bytes 17874944 | tf_op jit(solution)/shard_map/ihd,hde->ihe/dot_general | solution.py:47
  241.0 2.2 multiply_reduce_fusion
  243.3 3.1 multiply_convert_fusion
  246.4 1.7 copy-done.5
  248.1 3.8 fusion.17
  251.9 2.9 copy.46
  254.8 5.1 copy.50
  259.9 12.9 %select_convert_fusion = bf16[32,384,384]{2,1,0:T(8,128)(2,1)} fusion(pred[384,384]{1,0:T(8,128)(4,1)S(1)} %iota_compare_fusion, bf16[384,32,128]{0,2,1:T(8,128)(2,1)} %copy-done.5, bf16[384,32,128]{2,1,0:T(8,128)(2,1)} %bitcast.62), kind=kOutput, calls=%fused_computation.2 | convolution fusion | flops 1217396736 | bytes 15876096 | tf_op jit(solution)/shard_map/ihe,jhe->hij/dot_general | solution.py:62
  272.8 10.5 %fusion.24 = f32[32,384,128]{1,2,0:T(8,128)} fusion(bf16[32,384,384]{2,1,0:T(8,128)(2,1)} %select_convert_fusion, bf16[384,32,128]{0,2,1:T(8,128)(2,1)} %copy-done.8), kind=kOutput, calls=%fused_computation.38 | convolution fusion | flops 1207959552 | bytes 18874368 | tf_op jit(solution)/shard_map/hij,jhd->ihd/dot_general | solution.py:64
  283.3 5.6 %fusion.1 = bf16[384,32,128]{0,2,1:T(8,128)(2,1)} fusion(f32[32,384,128]{1,2,0:T(8,128)} %fusion.24, bf16[384,32,128]{0,2,1:T(8,128)(2,1)S(1)} %copy-done.6, f32[32,128,128]{2,1,0:T(8,128)S(1)} %get-tuple-element.194), kind=kOutput, calls=%fused_computation.7 | convolution fusion | flops 406323200 | bytes 14680064 | tf_op jit(solution)/shard_map/ihe,hde->ihd/dot_general | solution.py:65
  288.9 4.8 copy.51
  293.7 40.7 %psum.7 = f32[4096]{0:T(1024)} all-reduce(f32[4096]{0:T(1024)S(1)} %bitcast.80), channel_id=1, replica_groups=mesh['dp'=2,'ctx'=16] {'dp','ctx'}, use_global_device_ids=true, to_apply=%region_7.8 | all-reduce | flops 4096 | bytes 32768 | tf_op jit(solution)/shard_map/psum | solution.py:76
  334.4 89.7 %all-gather.7.cloned.1.call-done = f32[512,128,128]{2,1,0:T(8,128)} async-done(((f32[32,128,128]{2,1,0:T(8,128)}), f32[512,128,128]{2,1,0:T(8,128)}) %all-gather.7.cloned.1.call-update) | async-done | bytes 33554448 | tf_op jit(solution)/shard_map/all_gather | solution.py:14
  424.1 37.4 %while.31 = (s32[]{:T(128)}, f32[32,128,128]{2,1,0:T(8,128)S(1)}, s32[]{:T(128)}, f32[16,32,128,128]{3,2,1,0:T(8,128)}, s32[]{:T(128)}, /*index=5*/s32[]{:T(128)}, s32[]{:T(128)}, s32[]{:T(128)}) while((s32[]{:T(128)}, f32[32,128,128]{2,1,0:T(8,128)S(1)}, s32[]{:T(128)}, f32[16,32,128,128]{3,2,1,0:T(8,128)}, s32[]{:T(128)}, ...), condition=%wide.region_5.6_spmd.clone, body=%wide.region_4.5_spmd.clone.sunk | while | flops 1572872 | bytes 6291619 | solution.py:23
  424.1 2.3 add_select_fusion.5
  426.4 2.3 add_select_fusion.5
  428.8 2.3 add_select_fusion.5
  431.1 2.3 add_select_fusion.5
  433.5 2.3 add_select_fusion.5
  435.8 2.3 add_select_fusion.5
  438.1 2.3 add_select_fusion.5
  440.5 2.3 add_select_fusion.5
  442.8 2.3 add_select_fusion.5
  445.2 2.3 add_select_fusion.5
  447.5 2.3 add_select_fusion.5
  449.9 2.3 add_select_fusion.5
  452.2 2.3 add_select_fusion.5
  454.5 2.3 add_select_fusion.5
  456.9 2.3 add_select_fusion.5
  459.2 2.3 add_select_fusion.5
  461.6 5.7 %fusion.2 = f32[32,128,384]{2,1,0:T(8,128)S(1)} fusion(bf16[384,32,128]{2,1,0:T(8,128)(2,1)} %bitcast.70, f32[32,128,128]{2,1,0:T(8,128)S(1)} %get-tuple-element.195), kind=kOutput, calls=%fused_computation.15 | convolution fusion | flops 403177472 | bytes 11534336 | tf_op jit(solution)/shard_map/jhd,hde->jhe/dot_general | solution.py:73
  467.3 5.8 %fusion.7 = f32[32,128,384]{2,1,0:T(8,128)} fusion(bf16[384,32,128]{2,1,0:T(8,128)(2,1)S(1)} %bitcast.63, f32[32,128,128]{2,1,0:T(8,128)S(1)} %get-tuple-element.195), kind=kOutput, calls=%fused_computation.20 | convolution fusion | flops 403177472 | bytes 11534336 | tf_op jit(solution)/shard_map/jhe,hde->jhd/dot_general | solution.py:69
  473.1 7.9 %add_convert_fusion = bf16[32,128,384]{2,1,0:T(8,128)(2,1)} fusion(f32[32,128,384]{2,1,0:T(8,128)S(1)} %fusion.2, bf16[384,32,128]{0,2,1:T(8,128)(2,1)S(1)} %copy-done.7, bf16[32,384,384]{2,1,0:T(8,128)(2,1)} %select_convert_fusion.1), kind=kOutput, calls=%fused_computation.10 | convolution fusion | flops 1211105280 | bytes 22020096 | tf_op jit(solution)/shard_map/hij,ihe->jhe/dot_general | solution.py:72
  481.1 5.0 copy.53
  486.0 11.1 %fusion = bf16[384,32,128]{0,2,1:T(8,128)(2,1)} fusion(f32[32,128,384]{2,1,0:T(8,128)} %fusion.7, bf16[32,384,384]{2,1,0:T(8,128)(2,1)} %select_convert_fusion, bf16[384,32,128]{2,1,0:T(8,128)(2,1)S(1)} %bitcast.67), kind=kOutput, calls=%fused_computation.5 | convolution fusion | flops 1211105280 | bytes 22020096 | tf_op jit(solution)/shard_map/hij,ihd->jhd/dot_general | solution.py:68
  497.1 4.6 copy.52
  (31 shorter events, 0.2 us)
Async XLA Ops:
  7.2 188.5 %all-gather.5.cloned.1.call-start = ((), (), s32[]{:S(2)}) async-start(), calls=%async_computation | async-start | bytes 35651584 | tf_op jit(solution)/shard_map/all_gather | solution.py:14
  15.4 3.9 copy-start.8
  19.3 1.6 copy-start.1
  24.7 399.4 %all-gather.7.cloned.1.call-start = ((), (), s32[]{:S(2)}) async-start(), calls=%async_computation.1 | async-start | bytes 35651584 | tf_op jit(solution)/shard_map/all_gather | solution.py:14
  233.3 7.7 %slice-start = ((s8[6291456]{0:T(1024)(128)(4,1)}), s8[4194304]{0:T(1024)(128)(4,1)S(1)}, s32[]{:S(2)}) async-start(s8[6291456]{0:T(1024)(128)(4,1)} %bitcast.56), calls=%async_computation.2 | async-start | bytes 8388608
  233.3 7.7 %slice-start.1 = ((s8[6291456]{0:T(1024)(128)(4,1)}), s8[2097152]{0:T(1024)(128)(4,1)S(1)}, s32[]{:S(2)}) async-start(s8[6291456]{0:T(1024)(128)(4,1)} %bitcast.56), calls=%async_computation.3 | async-start | bytes 4194304
  233.3 7.7 %copy-start.9 = (f32[4096]{0:T(1024)S(1)}, f32[4096]{0:T(1024)}, u32[]{:S(2)}) copy-start(f32[4096]{0:T(1024)} %param.13) | copy-start | bytes 49156
  243.3 4.8 copy-start.3
  246.4 1.7 copy-start.5
  272.8 10.5 %copy-start.6 = (bf16[384,32,128]{0,2,1:T(8,128)(2,1)S(1)}, bf16[384,32,128]{0,2,1:T(8,128)(2,1)}, u32[]{:S(2)}) copy-start(bf16[384,32,128]{0,2,1:T(8,128)(2,1)} %copy-done.5) | copy-start | bytes 9437188
  288.9 135.2 %copy-start = (f32[32,128,128]{2,1,0:T(8,128)S(1)}, f32[32,128,128]{2,1,0:T(8,128)}, u32[]{:S(2)}) copy-start(f32[32,128,128]{2,1,0:T(8,128)} %custom-call.1) | copy-start | bytes 6291460
  461.5 5.8 %copy-start.2 = (bf16[48,8,32,128]{3,2,1,0:T(8,128)(2,1)S(1)}, bf16[48,8,32,128]{3,2,1,0:T(8,128)(2,1)}, u32[]{:S(2)}) copy-start(bf16[48,8,32,128]{3,2,1,0:T(8,128)(2,1)} %copy-done.1) | copy-start | bytes 9437188
  467.3 5.8 %copy-start.7 = (bf16[384,32,128]{0,2,1:T(8,128)(2,1)S(1)}, bf16[384,32,128]{0,2,1:T(8,128)(2,1)}, u32[]{:S(2)}) copy-start(bf16[384,32,128]{0,2,1:T(8,128)(2,1)} %copy-done.5) | copy-start | bytes 9437188
  481.1 5.0 copy-start.4
Sparse Core Ops, SparseCore 0:
  24.8 170.7 all-gather.4
  254.9 169.1 all-gather.6
where the time goes:
time: 514 us; the launch traced here: 509 us
  waiting for transfers between devices  225 us (44%)
  matrix products  100 us (19%)
  other arithmetic  79.4 us (15%)
  local copies, waits for them, and re-layouts  47.6 us (9%)
  blocking collectives  40.7 us (8%)
  between operations  14.5 us (3%)
    all_gather x2, waiting for transfers between devices, entering(): everything = lax.all_gather(x, axis)  225 us
    select_n x32, other arithmetic, lap(): return jnp.where(reached, new, before)  74 us
    psum x1, blocking collectives, body(): grad_gain = lax.psum(gain_term.reshape(heads * HD), ('dp', 'ctx'))  40.7 us
    unnamed x31, local copies, waits for them, and re-layouts  35.5 us
    dot_general x1, matrix products, body(): jnp.einsum('ihd,jhd->hij', query, key_rows, preferred_element_type=jnp.fl...  13.7 us
    dot_general x1, matrix products, body(): jnp.einsum('ihe,jhe->hij', dattn, value, preferred_element_type=jnp.float32)  12.9 us
    dot_general x1, matrix products, body(): jnp.einsum('hij,jhe->ihe', scores, value, preferred_element_type=jnp.floa...  11.6 us
    dot_general x1, matrix products, body(): jnp.einsum('hij,ihd->jhd', dscore, query, preferred_element_type=jnp.floa...  11.1 us
  transfers between devices with their start and end apart: 2, of which 2 were waited for; matrix products, arithmetic and copies ran while one was open for 15% of the time, Pallas kernels for 0%

commit v1 on v0

v1 whole, which is shorter than its diff:
```python
import functools

import jax
import jax.numpy as jnp
from jax import lax
from jax.experimental import pallas as pl
from jax.experimental.pallas import tpu as pltpu
from jax.sharding import PartitionSpec as P

HD = 128
PW = 2 * HD
EPS = 1e-06
F32 = jnp.float32
BF16 = jnp.bfloat16
MESH = pl.DeviceIdType.MESH

LAG_FWD = 2
LAG_GY = 4
LAG_GZ = 6
LAG_STEP = 4
LAG_FIN = 2
LAG_PRO = 3


def nt(a, b):
    return lax.dot_general(a, b, (((1,), (1,)), ((), ())), preferred_element_type=F32)


def nn(a, b):
    return lax.dot_general(a, b, (((1,), (0,)), ((), ())), preferred_element_type=F32)


def tn(a, b):
    return lax.dot_general(a, b, (((0,), (0,)), ((), ())), preferred_element_type=F32)


def kernel(
    ndp, nctx, pairs,
    q_hbm, k_hbm, v_hbm, g_hbm, gain_ref,
    o_hbm, gq_hbm, gk_hbm, gv_hbm, gg_ref,
    qb, kb, vb, gb, gki, gvi,
    s_all, x_in, c_out, y_in, e_in, e_out, p_out, p_all,
    t_all, tx_in, tc_out, ty_in, te_in, te_out, tp_out, tp_all,
    gsum, grecv,
    io_sem, send_sem, recv_sem, gs_sem, gr_sem,
):
    dp = lax.axis_index("dp")
    me = lax.axis_index("ctx")
    c = lax.rem(me, 2)
    y = lax.rem(me // 2, 2)
    z = me // 4
    nz = nctx // 4
    sib = (dp, me + 1 - 2 * c)
    ypeer = (dp, me + 2 - 4 * y)
    up = (dp, lax.min(me + 4, nctx - 1))
    down = (dp, lax.max(me - 4, 0))
    length = qb.shape[1]

    steps = []
    bit = 1
    while bit < ndp:
        steps.append((dp + bit - 2 * bit * lax.rem(dp // bit, 2), me))
        bit *= 2
    n_dp = len(steps)
    bit = 1
    while bit < nctx:
        steps.append((dp, me + bit - 2 * bit * lax.rem(me // bit, 2)))
        bit *= 2

    def loads(p):
        cols = pl.ds(pl.multiple_of(p * PW, PW), PW)
        return [
            pltpu.make_async_copy(h.at[0, :, cols], b.at[p], io_sem.at[i, p])
            for i, (h, b) in enumerate(((k_hbm, kb), (v_hbm, vb), (q_hbm, qb), (g_hbm, gb)))
        ]

    def stores(p):
        cols = pl.ds(pl.multiple_of(p * PW, PW), PW)
        return [
            pltpu.make_async_copy(b.at[p], h.at[0, :, cols], io_sem.at[i, p])
            for i, (h, b) in enumerate(((gk_hbm, kb), (gv_hbm, vb), (gq_hbm, qb), (o_hbm, gb)))
        ]

    def hop(kind, src, dst, p, to):
        return pltpu.make_async_remote_copy(
            src_ref=src, dst_ref=dst, send_sem=send_sem.at[kind], recv_sem=recv_sem.at[kind, p],
            device_id=to, device_id_type=MESH,
        )

    def load_kv(p, _):
        for copy in loads(p)[:2]:
            copy.start()
        return 0

    def load_qg(p, _):
        for copy in loads(p)[2:]:
            copy.start()
        return 0

    lax.fori_loop(0, pairs, load_kv, 0)
    lax.fori_loop(0, pairs, load_qg, 0)

    barrier = pltpu.get_barrier_semaphore()
    greet = [sib, ypeer] + steps[:n_dp] + steps[n_dp + 3:]
    for other in greet:
        pl.semaphore_signal(barrier, inc=1, device_id=other, device_id_type=MESH)

    @pl.when(z < nz - 1)
    def _():
        pl.semaphore_signal(barrier, inc=1, device_id=up, device_id_type=MESH)

    @pl.when(z > 0)
    def _():
        pl.semaphore_signal(barrier, inc=1, device_id=down, device_id_type=MESH)

    expected = len(greet) + lax.min(z, 1) + lax.min(nz - 1 - z, 1)
    pl.semaphore_wait(barrier, expected)

    @pl.when(z == 0)
    def _():
        e_in[...] = jnp.zeros_like(e_in)

    @pl.when(z == nz - 1)
    def _():
        te_in[...] = jnp.zeros_like(te_in)

    def to_chip(p, kind, all_ref, in_ref):
        return hop(kind, all_ref.at[1 - c, p], in_ref.at[p], p, sib)

    def chip_total(p, kind, all_ref, in_ref, out_ref, y_ref):
        to_chip(p, kind, all_ref, in_ref).wait_recv()
        out_ref[p] = all_ref[c, p] + in_ref[p]
        hop(kind + 1, out_ref.at[p], y_ref.at[p], p, ypeer).start()

    def along(p, kind, all_ref, in_ref, out_ref, y_ref, e_ref, eo_ref, po_ref, pa_ref, reverse):
        first = nz - 1 if reverse else 0
        last = nz - 1 - first
        to = down if reverse else up
        hop(kind + 1, out_ref.at[p], y_ref.at[p], p, ypeer).wait_recv()

        @pl.when(z != first)
        def _():
            hop(kind + 2, eo_ref.at[p], e_ref.at[p], p, to).wait_recv()

        entering = e_ref[p]
        across = y_ref[p]

        @pl.when(z != last)
        def _():
            eo_ref[p] = entering + (out_ref[p] + across)
            hop(kind + 2, eo_ref.at[p], e_ref.at[p], p, to).start()

        has_y = (y == 0) if reverse else (y == 1)
        mine_later = (c == 0) if reverse else (c == 1)
        base = entering + jnp.where(has_y, across, 0.0)
        po_ref[p] = base + jnp.where(mine_later, 0.0, all_ref[c, p])
        hop(kind + 3, po_ref.at[p], pa_ref.at[c, p], p, sib).start()
        pa_ref[c, p] = base + jnp.where(mine_later, in_ref[p], 0.0)

    fwd = (0, s_all, x_in, c_out, y_in)
    bwd = (4, t_all, tx_in, tc_out, ty_in)

    def prologue(t, _):
        @pl.when(t < pairs)
        def _():
            for copy in loads(t)[:2]:
                copy.wait()
            for j in range(2):
                at = slice(j * HD, (j + 1) * HD)
                s_all[j, t] = tn(kb[t, :, at], vb[t, :, at])
            to_chip(t, 0, s_all, x_in).start()

        @pl.when(t >= LAG_PRO)
        def _():
            chip_total(t - LAG_PRO, *fwd)
        return 0

    lax.fori_loop(0, pairs + LAG_PRO, prologue, 0)

    def forward(p):
        for copy in loads(p)[2:]:
            copy.wait()
        hop(3, p_out.at[p], p_all.at[1 - c, p], p, sib).wait_recv()
        row = lax.broadcasted_iota(jnp.int32, (length, length), 0)
        col = lax.broadcasted_iota(jnp.int32, (length, length), 1)
        causal = row >= col
        kept = []
        for j in range(2):
            at = slice(j * HD, (j + 1) * HD)
            lanes = pl.ds(pl.multiple_of(p * PW + j * HD, HD), HD)
            query, key_rows, value = qb[p, :, at], kb[p, :, at], vb[p, :, at]
            prefix = p_all[j, p].astype(BF16)
            scores = jnp.where(causal, nt(query, key_rows), 0.0).astype(BF16)
            attended = nn(scores, value) + nn(query, prefix)
            inverse = lax.rsqrt(jnp.mean(attended * attended, axis=-1, keepdims=True) + EPS)
            normed = attended * inverse
            gain = gain_ref[:, lanes]
            grad = gb[p, :, at].astype(F32)
            gsum[0, :, lanes] = jnp.sum(grad * normed, axis=0, keepdims=True)
            scaled = grad * gain
            dattn = (
                inverse * (scaled - normed * jnp.mean(scaled * normed, axis=-1, keepdims=True))
            ).astype(BF16)
            gb[p, :, at] = (normed * gain).astype(BF16)
            t_all[j, p] = tn(query, dattn)
            kept.append((query, key_rows, value, prefix, scores, dattn))
        to_chip(p, 4, t_all, tx_in).start()
        for j in range(2):
            at = slice(j * HD, (j + 1) * HD)
            query, key_rows, value, prefix, scores, dattn = kept[j]
            dscore = jnp.where(causal, nt(dattn, value), 0.0).astype(BF16)
            grad_q = nn(dscore, key_rows) + nt(dattn, prefix)
            gki[p, :, at] = tn(dscore, query)
            gvi[p, :, at] = tn(scores, dattn)
            qb[p, :, at] = grad_q.astype(BF16)
        for copy in stores(p)[2:]:
            copy.start()

    def final(p):
        hop(7, tp_out.at[p], tp_all.at[1 - c, p], p, sib).wait_recv()
        for j in range(2):
            at = slice(j * HD, (j + 1) * HD)
            key_rows, value = kb[p, :, at], vb[p, :, at]
            suffix = tp_all[j, p].astype(BF16)
            kb[p, :, at] = (gki[p, :, at] + nt(value, suffix)).astype(BF16)
            vb[p, :, at] = (gvi[p, :, at] + nn(key_rows, suffix)).astype(BF16)
        for copy in stores(p)[:2]:
            copy.start()

    def gain_hop(i):
        return pltpu.make_async_remote_copy(
            src_ref=gsum.at[i], dst_ref=grecv.at[i], send_sem=gs_sem.at[i], recv_sem=gr_sem.at[i],
            device_id=steps[i], device_id_type=MESH,
        )

    lag_gz = LAG_GZ + LAG_STEP * (nz - 1 - z)
    gain_at = pairs + LAG_FWD
    total = max(
        pairs + LAG_GZ + LAG_STEP * (nz - 1) + LAG_FIN,
        gain_at + 2 * len(steps) + 1,
    )

    def guarded(p, stage):
        @pl.when(jnp.logical_and(p >= 0, p < pairs))
        def _():
            stage(p)

    def main(t, _):
        guarded(t, lambda p: along(p, *fwd, e_in, e_out, p_out, p_all, False))
        guarded(t - LAG_FWD, forward)
        guarded(t - LAG_GY, lambda p: chip_total(p, *bwd))
        guarded(t - lag_gz, lambda p: along(p, *bwd, te_in, te_out, tp_out, tp_all, True))
        guarded(t - lag_gz - LAG_FIN, final)
        for i in range(len(steps) + 1):
            @pl.when(t == gain_at + 2 * i)
            def _():
                if i > 0:
                    gain_hop(i - 1).wait_recv()
                    gsum[i] = gsum[i - 1] + grecv[i - 1]
                if i < len(steps):
                    gain_hop(i).start()
        return 0

    lax.fori_loop(0, total, main, 0)
    gg_ref[...] = gsum[len(steps)]

    for i in range(len(steps)):
        gain_hop(i).wait_send()
    for kind, all_ref, in_ref, out_ref, y_ref, eo_ref, e_ref, po_ref, pa_ref in (
        (*fwd, e_out, e_in, p_out, p_all),
        (*bwd, te_out, te_in, tp_out, tp_all),
    ):
        hop(kind, all_ref.at[1 - c], in_ref, 0, sib).wait_send()
        hop(kind + 1, out_ref, y_ref, 0, ypeer).wait_send()
        reverse = kind == 4

        @pl.when(z != (0 if reverse else nz - 1))
        def _():
            hop(kind + 2, eo_ref, e_ref, 0, down if reverse else up).wait_send()

        hop(kind + 3, po_ref, pa_ref.at[c], 0, sib).wait_send()

    def finish(p, _):
        for copy in stores(p):
            copy.wait()
        return 0

    lax.fori_loop(0, pairs, finish, 0)


def body(ndp, nctx, queries, keys, values, out_grad, gain):
    _, length, width = queries.shape
    pairs = width // PW
    nsteps = (ndp - 1).bit_length() + (nctx - 1).bit_length()
    tile = pltpu.VMEM((pairs, length, PW), BF16)
    wide = pltpu.VMEM((pairs, length, PW), F32)
    one = pltpu.VMEM((pairs, HD, HD), F32)
    two = pltpu.VMEM((2, pairs, HD, HD), F32)
    states = [two, one, one, one, one, one, one, two]
    hbm = pl.BlockSpec(memory_space=pl.ANY)
    vmem = pl.BlockSpec(memory_space=pltpu.VMEM)
    big = jax.ShapeDtypeStruct(queries.shape, BF16)
    out = pl.pallas_call(
        functools.partial(kernel, ndp, nctx, pairs),
        out_shape=(big, big, big, big, jax.ShapeDtypeStruct((1, width), F32)),
        in_specs=[hbm, hbm, hbm, hbm, vmem],
        out_specs=(hbm, hbm, hbm, hbm, vmem),
        scratch_shapes=[
            tile, tile, tile, tile, wide, wide, *states, *states,
            pltpu.VMEM((nsteps + 1, 1, width), F32),
            pltpu.VMEM((nsteps, 1, width), F32),
            pltpu.SemaphoreType.DMA((4, pairs)),
            pltpu.SemaphoreType.DMA((8,)),
            pltpu.SemaphoreType.DMA((8, pairs)),
            pltpu.SemaphoreType.DMA((nsteps,)),
            pltpu.SemaphoreType.DMA((nsteps,)),
        ],
        compiler_params=pltpu.CompilerParams(
            collective_id=0, has_side_effects=True, vmem_limit_bytes=56 << 20
        ),
        name="lightning",
    )(queries, keys, values, out_grad, gain.reshape(1, width))
    return (*out[:4], out[4].reshape(width))


def solution(mesh):
    split = P("dp", "ctx", None)
    return jax.shard_map(
        functools.partial(body, mesh.shape["dp"], mesh.shape["ctx"]),
        mesh=mesh,
        in_specs=(split, split, split, split, P()),
        out_specs=(split, split, split, split, P()),
        check_vma=False,
    )
```

time: 514 us -> 99 us (0.19)
  waiting for transfers between devices: 225 us -> 0 us
  matrix products: 100 us -> 0 us
  Pallas kernels: 0 us -> 85.5 us
  other arithmetic: 79.4 us -> 0 us
  blocking collectives: 40.7 us -> 0 us
  local copies, waits for them, and re-layouts: 47.6 us -> 12.4 us
  between operations: 14.5 us -> 0.65 us
    all_gather x2 -> x0, waiting for transfers between devices: 225 us -> none  [entering(): everything = lax.all_gather(x, axis)]
    dot_general x12 -> x0, matrix products: 100 us -> none  [the longest x1 13.7 us: body(): jnp.einsum('ihd,jhd->hij', query, key_rows, preferred_element_type=jnp.fl...]
    pallas_call x0 -> x1, Pallas kernels: none -> 85.5 us  [body(): pl.pallas_call(functools.partial(kernel, ndp, nctx, pairs), out_shape=(bi...]
    select_n x32 -> x0, other arithmetic: 74 us -> none  [lap(): return jnp.where(reached, new, before)]
    psum x1 -> x0, blocking collectives: 40.7 us -> none  [body(): grad_gain = lax.psum(gain_term.reshape(heads * HD), ('dp', 'ctx'))]
    unnamed x31 -> x13, local copies, waits for them, and re-layouts: 35.5 us -> 12.4 us
    convert_element_type x1 -> x0, local copies, waits for them, and re-layouts: 5.36 us -> none  [body(): grad_float = out_grad[0].reshape(length, heads, HD).astype(jnp.float32)]
  transfers between devices with their start and end apart: 2 -> 0, of which waited for: 2 -> 0; matrix products, arithmetic and copies ran while one was open for 15% -> 0% of each run, Pallas kernels for 0% -> 0%
where the time goes in v1:
time: 99 us; the launch traced here: 98.6 us
  Pallas kernels  85.5 us (86%)
  local copies, waits for them, and re-layouts  12.4 us (13%)
    pallas_call x1, Pallas kernels, body(): pl.pallas_call(functools.partial(kernel, ndp, nctx, pairs), out_shape=(bi...  85.5 us
    unnamed x13, local copies, waits for them, and re-layouts  12.4 us

profile of v1, /device:TPU:0, one launch (start us, length us, event | category | flops | bytes accessed | tf_op | source)
XLA Modules:
  0.0 98.6 jit_solution(13678232099513516097)
XLA Ops:
  0.6 85.5 %lightning.1 = (bf16[1,384,4096]{2,1,0:T(8,128)(2,1)}, bf16[1,384,4096]{2,1,0:T(8,128)(2,1)}, bf16[1,384,4096]{2,1,0:T(8,128)(2,1)}, bf16[1,384,4096]{2,1,0:T(8,128)(2,1)}, f32[1,4096]{1,0:T(1,128)}) custom-call(bf16[1,384,4096]{2,1,0:T(8,128)(2,1)} %q_hbm.1, bf16[1,384,4096]{2,1,0:T(8,128)(2,1)} %k_hbm.1, bf16[1,384,4096]{2,1,0:T(8,128)(2,1)} %v_hbm.1, ...), custom_call_target="tpu_custom_call" | custom-call | tf_op jit(solution)/shard_map/lightning/pallas_call | solution.py:303
  86.2 0.0 copy-start.2
  86.2 4.1 %copy.15 = bf16[1,384,4096]{2,1,0:T(8,128)(2,1)} copy(bf16[1,384,4096]{2,1,0:T(8,128)(2,1)} %get-tuple-element.20) | data formatting | bytes 6291456
  90.2 0.0 copy-done.2
  90.2 0.0 copy-start.1
  90.2 1.7 %copy.16 = bf16[1,384,4096]{2,1,0:T(8,128)(2,1)} copy(bf16[1,384,4096]{2,1,0:T(8,128)(2,1)S(1)} %copy-done.2) | data formatting | bytes 6291456
  91.9 1.4 %copy-done.1 = bf16[1,384,4096]{2,1,0:T(8,128)(2,1)S(1)} copy-done((bf16[1,384,4096]{2,1,0:T(8,128)(2,1)S(1)}, bf16[1,384,4096]{2,1,0:T(8,128)(2,1)}, u32[]{:S(2)}) %copy-start.1) | copy-done | bytes 3145752
  93.3 0.0 copy-start
  93.3 1.7 %copy.17 = bf16[1,384,4096]{2,1,0:T(8,128)(2,1)} copy(bf16[1,384,4096]{2,1,0:T(8,128)(2,1)S(1)} %copy-done.1) | data formatting | bytes 6291456
  94.9 1.4 %copy-done = bf16[1,384,4096]{2,1,0:T(8,128)(2,1)S(1)} copy-done((bf16[1,384,4096]{2,1,0:T(8,128)(2,1)S(1)}, bf16[1,384,4096]{2,1,0:T(8,128)(2,1)}, u32[]{:S(2)}) %copy-start) | copy-done | bytes 3145752
  96.3 0.0 copy-start.3
  96.3 1.7 %copy.18 = bf16[1,384,4096]{2,1,0:T(8,128)(2,1)} copy(bf16[1,384,4096]{2,1,0:T(8,128)(2,1)S(1)} %copy-done) | data formatting | bytes 6291456
  98.0 0.0 copy-done.3
  98.0 0.6 copy.19
Async XLA Ops:
  86.2 4.1 %copy-start.2 = (bf16[1,384,4096]{2,1,0:T(8,128)(2,1)S(1)}, bf16[1,384,4096]{2,1,0:T(8,128)(2,1)}, u32[]{:S(2)}) copy-start(bf16[1,384,4096]{2,1,0:T(8,128)(2,1)} %get-tuple-element.21) | copy-start | bytes 9437188
  90.2 3.0 %copy-start.1 = (bf16[1,384,4096]{2,1,0:T(8,128)(2,1)S(1)}, bf16[1,384,4096]{2,1,0:T(8,128)(2,1)}, u32[]{:S(2)}) copy-start(bf16[1,384,4096]{2,1,0:T(8,128)(2,1)} %get-tuple-element.22) | copy-start | bytes 9437188
  93.3 3.0 %copy-start = (bf16[1,384,4096]{2,1,0:T(8,128)(2,1)S(1)}, bf16[1,384,4096]{2,1,0:T(8,128)(2,1)}, u32[]{:S(2)}) copy-start(bf16[1,384,4096]{2,1,0:T(8,128)(2,1)} %get-tuple-element.23) | copy-start | bytes 9437188
  96.3 1.7 %copy-start.3 = (f32[1,4096]{1,0:T(1,128)S(1)}, f32[1,4096]{1,0:T(1,128)}, u32[]{:S(2)}) copy-start(f32[1,4096]{1,0:T(1,128)} %get-tuple-element.14) | copy-start | bytes 49156

commit v2 on v1

--- a/solution.py
+++ b/solution.py
@@ -20,6 +20,7 @@
 LAG_STEP = 4
 LAG_FIN = 2
 LAG_PRO = 3
+LAG_TURN = 4
 
 
 def nt(a, b):
@@ -38,7 +39,7 @@
     ndp, nctx, pairs,
     q_hbm, k_hbm, v_hbm, g_hbm, gain_ref,
     o_hbm, gq_hbm, gk_hbm, gv_hbm, gg_ref,
-    qb, kb, vb, gb, gki, gvi,
+    qb, kb, vb, gb, kept, held,
     s_all, x_in, c_out, y_in, e_in, e_out, p_out, p_all,
     t_all, tx_in, tc_out, ty_in, te_in, te_out, tp_out, tp_all,
     gsum, grecv,
@@ -184,47 +185,75 @@
         row = lax.broadcasted_iota(jnp.int32, (length, length), 0)
         col = lax.broadcasted_iota(jnp.int32, (length, length), 1)
         causal = row >= col
-        kept = []
-        for j in range(2):
-            at = slice(j * HD, (j + 1) * HD)
-            lanes = pl.ds(pl.multiple_of(p * PW + j * HD, HD), HD)
-            query, key_rows, value = qb[p, :, at], kb[p, :, at], vb[p, :, at]
-            prefix = p_all[j, p].astype(BF16)
-            scores = jnp.where(causal, nt(query, key_rows), 0.0).astype(BF16)
-            attended = nn(scores, value) + nn(query, prefix)
-            inverse = lax.rsqrt(jnp.mean(attended * attended, axis=-1, keepdims=True) + EPS)
-            normed = attended * inverse
-            gain = gain_ref[:, lanes]
-            grad = gb[p, :, at].astype(F32)
-            gsum[0, :, lanes] = jnp.sum(grad * normed, axis=0, keepdims=True)
-            scaled = grad * gain
-            dattn = (
-                inverse * (scaled - normed * jnp.mean(scaled * normed, axis=-1, keepdims=True))
-            ).astype(BF16)
-            gb[p, :, at] = (normed * gain).astype(BF16)
-            t_all[j, p] = tn(query, dattn)
-            kept.append((query, key_rows, value, prefix, scores, dattn))
+        two = range(2)
+        at = [slice(j * HD, (j + 1) * HD) for j in two]
+        lanes = [pl.ds(pl.multiple_of(p * PW + j * HD, HD), HD) for j in two]
+        query = [qb[p, :, at[j]] for j in two]
+        key_rows = [kb[p, :, at[j]] for j in two]
+        value = [vb[p, :, at[j]] for j in two]
+        grad = [gb[p, :, at[j]].astype(F32) for j in two]
+        prefix = [p_all[j, p].astype(BF16) for j in two]
+        gain = [gain_ref[:, lanes[j]] for j in two]
+        scores = [jnp.where(causal, nt(query[j], key_rows[j]), 0.0).astype(BF16) for j in two]
+        attended = [
+            nn(
+                jnp.concatenate([scores[j], query[j]], axis=1),
+                jnp.concatenate([value[j], prefix[j]], axis=0),
+            )
+            for j in two
+        ]
+        inverse = [
+            lax.rsqrt(jnp.mean(attended[j] * attended[j], axis=-1, keepdims=True) + EPS) for j in two
+        ]
+        normed = [attended[j] * inverse[j] for j in two]
+        product = [grad[j] * normed[j] for j in two]
+        mean = [jnp.mean(product[j] * gain[j], axis=-1, keepdims=True) for j in two]
+        dattn = [
+            (inverse[j] * (grad[j] * gain[j] - normed[j] * mean[j])).astype(BF16) for j in two
+        ]
+        gstate = [tn(query[j], dattn[j]) for j in two]
+        for j in two:
+            t_all[j, p] = gstate[j]
         to_chip(p, 4, t_all, tx_in).start()
-        for j in range(2):
-            at = slice(j * HD, (j + 1) * HD)
-            query, key_rows, value, prefix, scores, dattn = kept[j]
-            dscore = jnp.where(causal, nt(dattn, value), 0.0).astype(BF16)
-            grad_q = nn(dscore, key_rows) + nt(dattn, prefix)
-            gki[p, :, at] = tn(dscore, query)
-            gvi[p, :, at] = tn(scores, dattn)
-            qb[p, :, at] = grad_q.astype(BF16)
-        for copy in stores(p)[2:]:
-            copy.start()
+        for j in two:
+            kept[p, :, at[j]] = dattn[j]
+            held[j, p] = scores[j]
+            gsum[0, :, lanes[j]] = jnp.sum(product[j], axis=0, keepdims=True)
+            gb[p, :, at[j]] = (normed[j] * gain[j]).astype(BF16)
+        stores(p)[3].start()
 
     def final(p):
         hop(7, tp_out.at[p], tp_all.at[1 - c, p], p, sib).wait_recv()
-        for j in range(2):
-            at = slice(j * HD, (j + 1) * HD)
-            key_rows, value = kb[p, :, at], vb[p, :, at]
-            suffix = tp_all[j, p].astype(BF16)
-            kb[p, :, at] = (gki[p, :, at] + nt(value, suffix)).astype(BF16)
-            vb[p, :, at] = (gvi[p, :, at] + nn(key_rows, suffix)).astype(BF16)
-        for copy in stores(p)[:2]:
+        row = lax.broadcasted_iota(jnp.int32, (length, length), 0)
+        col = lax.broadcasted_iota(jnp.int32, (length, length), 1)
+        causal = row >= col
+        two = range(2)
+        at = [slice(j * HD, (j + 1) * HD) for j in two]
+        query = [qb[p, :, at[j]] for j in two]
+        key_rows = [kb[p, :, at[j]] for j in two]
+        value = [vb[p, :, at[j]] for j in two]
+        dattn = [kept[p, :, at[j]] for j in two]
+        prefix = [p_all[j, p].astype(BF16) for j in two]
+        suffix = [tp_all[j, p].astype(BF16) for j in two]
+        dscore = [jnp.where(causal, nt(dattn[j], value[j]), 0.0).astype(BF16) for j in two]
+        grad_v = [
+            (tn(held[j, p], dattn[j]) + nn(key_rows[j], suffix[j])).astype(BF16) for j in two
+        ]
+        grad_q = [
+            nn(
+                jnp.concatenate([dscore[j], dattn[j]], axis=1),
+                jnp.concatenate([key_rows[j], prefix[j].T], axis=0),
+            ).astype(BF16)
+            for j in two
+        ]
+        grad_k = [
+            (tn(dscore[j], query[j]) + nt(value[j], suffix[j])).astype(BF16) for j in two
+        ]
+        for j in two:
+            qb[p, :, at[j]] = grad_q[j]
+            kb[p, :, at[j]] = grad_k[j]
+            vb[p, :, at[j]] = grad_v[j]
+        for copy in stores(p)[:3]:
             copy.start()
 
     def gain_hop(i):
@@ -234,9 +263,11 @@
         )
 
     lag_gz = LAG_GZ + LAG_STEP * (nz - 1 - z)
-    gain_at = pairs + LAG_FWD
+    after = pairs + LAG_FWD
+    lag_fin = lax.max(lag_gz + LAG_FIN, after + LAG_TURN * (z // (nz - 1)))
+    gain_at = after
     total = max(
-        pairs + LAG_GZ + LAG_STEP * (nz - 1) + LAG_FIN,
+        pairs + max(LAG_GZ + LAG_STEP * (nz - 1) + LAG_FIN, after + LAG_TURN),
         gain_at + 2 * len(steps) + 1,
     )
 
@@ -250,7 +281,7 @@
         guarded(t - LAG_FWD, forward)
         guarded(t - LAG_GY, lambda p: chip_total(p, *bwd))
         guarded(t - lag_gz, lambda p: along(p, *bwd, te_in, te_out, tp_out, tp_all, True))
-        guarded(t - lag_gz - LAG_FIN, final)
+        guarded(t - lag_fin, final)
         for i in range(len(steps) + 1):
             @pl.when(t == gain_at + 2 * i)
             def _():
@@ -288,12 +319,34 @@
     lax.fori_loop(0, pairs, finish, 0)
 
 
+def settle(chunks, *refs):
+    sources, total, targets, result, stage, sems = refs[:4], refs[4], refs[5:9], refs[9], refs[10], refs[11]
+    rows = stage.shape[1]
+
+    def pair(i):
+        a, r = i // chunks, pl.ds((i % chunks) * rows, rows)
+        return (
+            pltpu.make_async_copy(sources[a].at[0, r], stage.at[i], sems.at[i]),
+            pltpu.make_async_copy(stage.at[i], targets[a].at[0, r], sems.at[i]),
+        )
+
+    for i in range(4 * chunks):
+        pair(i)[0].start()
+    result[...] = total[...]
+    for i in range(4 * chunks):
+        inward, outward = pair(i)
+        inward.wait()
+        outward.start()
+    for i in range(4 * chunks):
+        pair(i)[1].wait()
+
+
 def body(ndp, nctx, queries, keys, values, out_grad, gain):
     _, length, width = queries.shape
     pairs = width // PW
     nsteps = (ndp - 1).bit_length() + (nctx - 1).bit_length()
     tile = pltpu.VMEM((pairs, length, PW), BF16)
-    wide = pltpu.VMEM((pairs, length, PW), F32)
+    square = pltpu.VMEM((2, pairs, length, length), BF16)
     one = pltpu.VMEM((pairs, HD, HD), F32)
     two = pltpu.VMEM((2, pairs, HD, HD), F32)
     states = [two, one, one, one, one, one, one, two]
@@ -306,7 +359,7 @@
         in_specs=[hbm, hbm, hbm, hbm, vmem],
         out_specs=(hbm, hbm, hbm, hbm, vmem),
         scratch_shapes=[
-            tile, tile, tile, tile, wide, wide, *states, *states,
+            tile, tile, tile, tile, tile, square, *states, *states,
             pltpu.VMEM((nsteps + 1, 1, width), F32),
             pltpu.VMEM((nsteps, 1, width), F32),
             pltpu.SemaphoreType.DMA((4, pairs)),
@@ -320,6 +373,19 @@
         ),
         name="lightning",
     )(queries, keys, values, out_grad, gain.reshape(1, width))
+    chunks = 4
+    out = pl.pallas_call(
+        functools.partial(settle, chunks),
+        out_shape=(big, big, big, big, jax.ShapeDtypeStruct((1, width), F32)),
+        in_specs=[hbm, hbm, hbm, hbm, vmem],
+        out_specs=(hbm, hbm, hbm, hbm, vmem),
+        scratch_shapes=[
+            pltpu.VMEM((4 * chunks, length // chunks, width), BF16),
+            pltpu.SemaphoreType.DMA((4 * chunks,)),
+        ],
+        compiler_params=pltpu.CompilerParams(vmem_limit_bytes=56 << 20),
+        name="settle",
+    )(*out)
     return (*out[:4], out[4].reshape(width))
 
 

time: 99 us -> 88.5 us (0.89)
  local copies, waits for them, and re-layouts: 12.4 us -> 0 us
  Pallas kernels: 85.5 us -> 87.5 us
    unnamed x13 -> x0, local copies, waits for them, and re-layouts: 12.4 us -> none
    pallas_call x0 -> x1, Pallas kernels: none -> 10.2 us  [body(): pl.pallas_call(functools.partial(settle, chunks), out_shape=(big, big, bi...]
    pallas_call x1, Pallas kernels: 85.5 us -> 77.3 us  [body(): pl.pallas_call(functools.partial(kernel, ndp, nctx, pairs), out_shape=(bi...]
where the time goes in v2:
time: 88.5 us; the launch traced here: 88.1 us
  Pallas kernels  87.5 us (99%)
    pallas_call x1, Pallas kernels, body(): pl.pallas_call(functools.partial(kernel, ndp, nctx, pairs), out_shape=(bi...  77.3 us
    pallas_call x1, Pallas kernels, body(): pl.pallas_call(functools.partial(settle, chunks), out_shape=(big, big, bi...  10.2 us

profile of v2, /device:TPU:0, one launch (start us, length us, event | category | flops | bytes accessed | tf_op | source)
XLA Modules:
  0.0 88.1 jit_solution(165877296857774198)
XLA Ops:
  0.6 77.3 %lightning.1 = (bf16[1,384,4096]{2,1,0:T(8,128)(2,1)}, bf16[1,384,4096]{2,1,0:T(8,128)(2,1)}, bf16[1,384,4096]{2,1,0:T(8,128)(2,1)}, bf16[1,384,4096]{2,1,0:T(8,128)(2,1)}, f32[1,4096]{1,0:T(1,128)}) custom-call(bf16[1,384,4096]{2,1,0:T(8,128)(2,1)} %q_hbm.1, bf16[1,384,4096]{2,1,0:T(8,128)(2,1)} %k_hbm.1, bf16[1,384,4096]{2,1,0:T(8,128)(2,1)} %v_hbm.1, ...), custom_call_target="tpu_custom_call" | custom-call | tf_op jit(solution)/shard_map/lightning/pallas_call | solution.py:356
  77.9 10.2 %settle.1 = (bf16[1,384,4096]{2,1,0:T(8,128)(2,1)}, bf16[1,384,4096]{2,1,0:T(8,128)(2,1)}, bf16[1,384,4096]{2,1,0:T(8,128)(2,1)}, bf16[1,384,4096]{2,1,0:T(8,128)(2,1)}, f32[1,4096]{1,0:T(1,128)}) custom-call(bf16[1,384,4096]{2,1,0:T(8,128)(2,1)} %get-tuple-element.15.refs_0_, bf16[1,384,4096]{2,1,0:T(8,128)(2,1)} %get-tuple-element.16.refs_1_, ...), custom_call_target="tpu_custom_call" | custom-call | tf_op jit(solution)/shard_map/settle/pallas_call | solution.py:377
